TPU v7x, 256 devices: a whole 4x4x8 slice. The times are simulated.
256 devices in a mesh: req: 32 (over z_hi, y, core), tp: 8 (over x, z_lo).
Axes of the slice: x: 4, y: 4, z: 8 (z_hi: 4, z_lo: 2; z = z_hi * 2 + z_lo), core: 2. Of those that a mesh axis runs over, the one named last changes fastest.
Arguments:
- suffix: bfloat16 [256, 64, 2048], P('tp', 'req')
- prefix_store: bfloat16 [32, 2048, 2, 2048], P('req', None, None, 'tp')
- prefix_owner: int32 [2], replicated, may hold values from 0 to 31, as said below
- prefix_group: int32 [64], replicated, may hold values from 0 to 1
- request_perm: int32 [64], replicated, may hold values from 0 to 63, each once
- suffix_len: int32 [64], replicated, may hold values from 1 to 256, 8192 in all
- ln_gain_attn: float32 [2048], replicated, may hold values from 0.1 to 1.9
- w_qkv: bfloat16 [2048, 3, 2048], P(None, None, 'tp'), may hold values from -0.125 to 0.125
- w_out_attn: bfloat16 [2048, 2048], P('tp'), may hold values from -2.390625 to 2.390625
- ln_gain_mlp: float32 [2048], replicated, may hold values from 0.1 to 1.9
- w_in: bfloat16 [2048, 5120], P(None, 'tp'), may hold values from -0.125 to 0.125
- w_down: bfloat16 [5120, 2048], P('tp'), may hold values from -0.078125 to 0.078125
Outputs:
- layer_out: bfloat16 [256, 64, 2048], P('tp', 'req')
Inputs may be any that keep to these rules, and one draw needn't show every extreme that they name: `prefix_owner`: 2 different block indices. `request_perm`: each request exactly once.
All inputs are finite; a program needn't handle non-finite values.
Results may differ from a plain program's by a relative error of at most 0.015.
The roundings to bfloat16 on the way count: a program that leaves them out, or rounds other values in their place, can miss the bound.
Values may be sent and summed in bfloat16 or wider, within the bound.
A program may use at most 64 MiB of HBM per device.

v0:
```python
import jax
import jax.numpy as jnp
from jax import lax
from jax.sharding import PartitionSpec as P

HD = 128


def from_root(block, axis, source):
    block = jnp.where(lax.axis_index(axis) == source, block, jnp.zeros_like(block))
    return lax.psum(block, axis)


def layer_norm(values, gain):
    values = values.astype(jnp.float32)
    center = values - jnp.mean(values, -1, keepdims=True)
    spread = jnp.mean(center * center, -1, keepdims=True)
    return center * lax.rsqrt(spread + 1e-05) * gain


def fetch_prefixes(prefix_store, prefix_owner):
    caches = []
    for group in range(prefix_owner.shape[0]):
        caches.append(from_root(prefix_store[0], "req", prefix_owner[group]))
    return jnp.stack(caches)


def project_rows(suffix, gain, w_qkv):
    gathered = lax.all_gather(suffix, "tp", axis=0, tiled=True)
    normed = layer_norm(gathered, gain).astype(jnp.bfloat16)
    projected = jnp.einsum(
        "srd,dce->srce", normed, w_qkv, preferred_element_type=jnp.float32
    ).astype(jnp.bfloat16)
    return (projected, gathered)


def attend(projected, cached, lengths):
    slot_count, slots_dev, _, local_width = projected.shape
    heads = local_width // HD
    prefix_rows = cached.shape[1]
    scale = HD ** (-0.5)
    queries = projected[:, :, 0].reshape(slot_count, slots_dev, heads, HD)
    keys_own = projected[:, :, 1].reshape(slot_count, slots_dev, heads, HD)
    values_own = projected[:, :, 2].reshape(slot_count, slots_dev, heads, HD)
    keys_pre = cached[:, :, 0].reshape(slots_dev, prefix_rows, heads, HD)
    values_pre = cached[:, :, 1].reshape(slots_dev, prefix_rows, heads, HD)
    scores_pre = (
        jnp.einsum("srhd,rphd->rhsp", queries, keys_pre, preferred_element_type=jnp.float32) * scale
    )
    scores_own = (
        jnp.einsum("srhd,trhd->rhst", queries, keys_own, preferred_element_type=jnp.float32) * scale
    )
    places = jnp.arange(slot_count, dtype=jnp.int32)
    visible = (places[None, None, None, :] <= places[None, None, :, None]) & (
        places[None, None, None, :] < lengths[:, None, None, None]
    )
    scores_own = jnp.where(visible, scores_own, -jnp.inf)
    highest = jnp.maximum(
        jnp.max(scores_pre, -1, keepdims=True), jnp.max(scores_own, -1, keepdims=True)
    )
    raised_pre = jnp.exp(scores_pre - highest)
    raised_own = jnp.exp(scores_own - highest)
    total = jnp.sum(raised_pre, -1, keepdims=True) + jnp.sum(raised_own, -1, keepdims=True)
    weights_pre = (raised_pre / total).astype(jnp.bfloat16)
    weights_own = (raised_own / total).astype(jnp.bfloat16)
    context = jnp.einsum(
        "rhsp,rphd->srhd", weights_pre, values_pre, preferred_element_type=jnp.float32
    )
    context = context + jnp.einsum(
        "rhst,trhd->srhd", weights_own, values_own, preferred_element_type=jnp.float32
    )
    return context.reshape(slot_count, slots_dev, local_width).astype(jnp.bfloat16)


def on_device(
    suffix,
    prefix_store,
    prefix_owner,
    prefix_group,
    request_perm,
    suffix_len,
    ln_gain_attn,
    w_qkv,
    w_out_attn,
    ln_gain_mlp,
    w_in,
    w_down,
):
    part_rows, slots_dev, _ = suffix.shape
    slots = lax.axis_index("req") * slots_dev + jnp.arange(slots_dev, dtype=jnp.int32)
    requests = jnp.take(request_perm, slots)
    lengths = jnp.take(suffix_len, requests)
    groups = jnp.take(prefix_group, requests)
    stacked = fetch_prefixes(prefix_store, prefix_owner)
    projected, gathered = project_rows(suffix, ln_gain_attn, w_qkv)
    cached = jnp.take(stacked, groups, axis=0)
    context = attend(projected, cached, lengths)
    first_row = lax.axis_index("tp") * part_rows
    block = context
    attention = lax.psum_scatter(
        jnp.einsum("srk,kd->srd", block, w_out_attn, preferred_element_type=jnp.float32).astype(
            jnp.bfloat16
        ),
        "tp",
        scatter_dimension=0,
        tiled=True,
    ).astype(jnp.float32)
    hidden = (suffix.astype(jnp.float32) + attention).astype(jnp.bfloat16)
    normed = layer_norm(hidden, ln_gain_mlp).astype(jnp.bfloat16)
    product = jnp.einsum(
        "srd,df->srf",
        lax.all_gather(normed, "tp", axis=0, tiled=True),
        w_in,
        preferred_element_type=jnp.float32,
    )
    inner = jax.nn.gelu(product, approximate=False).astype(jnp.bfloat16)
    block = inner
    down = lax.psum_scatter(
        jnp.einsum("srf,fd->srd", block, w_down, preferred_element_type=jnp.float32).astype(
            jnp.bfloat16
        ),
        "tp",
        scatter_dimension=0,
        tiled=True,
    ).astype(jnp.float32)
    places = first_row + jnp.arange(part_rows, dtype=jnp.int32)
    valid = places[:, None] < lengths[None, :]
    return jnp.where(valid[:, :, None], hidden.astype(jnp.float32) + down, 0.0).astype(jnp.bfloat16)


def solution(mesh):
    placed = (
        P("tp", "req", None),
        P("req", None, None, "tp"),
        P(),
        P(),
        P(),
        P(),
        P(),
        P(None, None, "tp"),
        P("tp", None),
        P(),
        P(None, "tp"),
        P("tp", None),
    )
    return jax.shard_map(
        on_device, mesh=mesh, in_specs=placed, out_specs=P("tp", "req", None), check_vma=False
    )
```

profile of v0, /device:TPU:16, one launch (start us, length us, event | category | flops | bytes accessed | tf_op | source)
XLA Modules:
  0.0 554.6 jit_solution(3519037379020641564)
XLA Ops:
  7.4 0.7 all-gather.3.cloned.1.call-update
  8.1 0.0 all-reduce.3.cloned.1.call-start
  8.1 1.4 fusion.112
  10.8 4.0 broadcast_select_fusion
  14.8 0.0 reduce-scatter.3.cloned.1.call-start
  14.9 0.5 copy-done.2
  15.5 0.6 gather_fusion.2
  16.1 0.6 gather_fusion.4
  16.8 0.6 gather_fusion.3
  17.5 0.1 iota_compare_fusion.1
  17.6 0.1 broadcast_and_fusion
  17.7 49.8 %all-gather.3.cloned.1.call-done = bf16[256,2,2048]{2,1,0:T(2,128)(2,1)} async-done(((bf16[32,2,2048]{2,1,0:T(2,128)(2,1)}), bf16[256,2,2048]{2,1,0:T(2,128)(2,1)}) %all-gather.3.cloned.1.call-update) | async-done | bytes 2097168 | tf_op jit(solution)/shard_map/all_gather | solution.py:29
  67.5 3.5 convert_reduce_fusion
  71.0 2.9 fusion.3
  73.9 3.3 fusion.12
  77.2 1.9 fusion.14
  79.1 0.8 fusion.111
  79.8 0.4 fusion.113
  80.2 246.9 %all-reduce.3.cloned.1.call-done = (bf16[1,2048,2,256]{3,1,2,0:T(8,128)(2,1)}, bf16[1,2048,2,256]{3,1,2,0:T(8,128)(2,1)}) async-done(((bf16[1,2048,2,256]{3,1,2,0:T(8,128)(2,1)}, bf16[1,2048,2,256]{3,1,2,0:T(8,128)(2,1)}), (bf16[1,2048,2,256]{3,1,2,0:T(8,128)(2,1)}, bf16[1,2048,2,256]{3,1,2,0:T(8,128)(2,1)})) %all-reduce.3.cloned.1.call-update) | async-done | bytes 4194320 | tf_op jit(solution)/shard_map/psum | solution.py:11
  327.1 1.9 constant_dynamic-update-slice_fusion.1
  328.9 0.3 copy-done.6
  329.3 0.1 constant_dynamic-update-slice_fusion
  329.4 2.2 fusion.110
  331.6 2.3 gather_fusion.1
  333.9 3.6 gather_fusion
  337.5 2.8 maximum_select_fusion
  340.3 1.6 fusion.109
  341.9 2.5 copy.50
  344.4 2.9 copy.53
  347.4 1.4 multiply_reduce_fusion
  348.8 1.6 fusion
  350.4 0.2 fusion.31
  350.6 2.8 fusion.6
  353.5 0.3 fusion.29
  353.8 0.9 copy-done.8
  354.7 2.1 convolution_convert_fusion
  356.8 0.0 all-gather.5.cloned.1.call-start
  356.8 65.7 %reduce-scatter.3.cloned.1.call-done = bf16[32,2,2048]{2,0,1:T(8,128)(2,1)} async-done(((bf16[256,2,2048]{2,0,1:T(8,128)(2,1)}), bf16[32,2,2048]{2,0,1:T(8,128)(2,1)}) %reduce-scatter.3.cloned.1.call-update) | async-done | bytes 262160 | tf_op jit(solution)/shard_map/reduce_scatter | solution.py:100
  422.5 1.1 convert_reduce_fusion.1
  423.7 0.2 fusion.66
  423.9 0.9 fusion.68
  424.8 54.1 %all-gather.5.cloned.1.call-done = bf16[256,2,2048]{2,0,1:T(8,128)(2,1)} async-done(((bf16[32,2,2048]{2,0,1:T(8,128)(2,1)}), bf16[256,2,2048]{2,0,1:T(8,128)(2,1)}) %all-gather.5.cloned.1.call-update) | async-done | bytes 2097168 | tf_op jit(solution)/shard_map/all_gather | solution.py:112
  478.9 4.4 fusion.74
  483.3 7.7 %convolution_convert_fusion.1 = bf16[256,2,2048]{2,0,1:T(8,128)(2,1)} fusion(bf16[640,2048]{1,0:T(8,128)(2,1)} %param.25, f32[256,2,640]{2,0,1:T(8,128)S(1)} %get-tuple-element.29, u8[256,640]{1,0:T(8,128)(4,1)S(1)} %get-tuple-element.7, u8[256,640]{1,0:T(8,128)(4,1)S(1)} %get-tuple-element.6), kind=kOutput, calls=%fused_computation.21 | convolution fusion | flops 1366163456 | bytes 6356992 | tf_op jit(solution)/shard_map/srf,fd->srd/dot_general | solution.py:119
  491.1 0.1 broadcast_compare_fusion
  491.2 54.3 %reduce-scatter.5.cloned.1.call-done = bf16[32,2,2048]{2,0,1:T(8,128)(2,1)} async-done(((bf16[256,2,2048]{2,0,1:T(8,128)(2,1)}), bf16[32,2,2048]{2,0,1:T(8,128)(2,1)}) %reduce-scatter.5.cloned.1.call-update) | async-done | bytes 262160 | tf_op jit(solution)/shard_map/reduce_scatter | solution.py:118
  545.5 1.0 fusion.70
  546.5 1.0 copy.60
  (44 shorter events, 0.3 us)
Async XLA Ops:
  7.4 69.8 %copy-start = (bf16[2048,3,256]{2,0,1:T(8,128)(2,1)S(1)}, bf16[2048,3,256]{2,0,1:T(8,128)(2,1)}, u32[]{:S(2)}) copy-start(bf16[2048,3,256]{2,0,1:T(8,128)(2,1)} %param.21) | copy-start | bytes 9437188
  7.4 60.1 %all-gather.3.cloned.1.call-start = ((), (), s32[]{:S(2)}) async-start(), calls=%async_computation.2 | async-start | bytes 2359296 | tf_op jit(solution)/shard_map/all_gather | solution.py:29
  8.1 319.0 %all-reduce.3.cloned.1.call-start = ((), (), s32[]{:S(2)}) async-start(), calls=%async_computation.6 | async-start | bytes 8388608 | tf_op jit(solution)/shard_map/psum | solution.py:11
  14.8 0.7 copy-start.2
  14.8 1.3 copy-start.3
  14.8 2.0 copy-start.4
  14.8 407.7 %reduce-scatter.3.cloned.1.call-start = ((), (), s32[]{:S(2)}) async-start(), calls=%async_computation.3 | async-start | bytes 2359296 | tf_op jit(solution)/shard_map/reduce_scatter | solution.py:100
  17.7 56.2 %copy-start.11 = (f32[2048]{0:T(1024)S(1)}, f32[2048]{0:T(1024)}, u32[]{:S(2)}) copy-start(f32[2048]{0:T(1024)} %param.20) | copy-start | bytes 24580
  67.5 3.5 copy-start.5
  327.1 2.2 copy-start.6
  348.8 1.8 copy-start.7
  350.6 2.8 copy-start.10
  353.5 1.2 copy-start.8
  354.7 67.8 %copy-start.9 = (bf16[32,2,2048]{2,1,0:T(2,128)(2,1)S(1)}, bf16[32,2,2048]{2,1,0:T(2,128)(2,1)}, u32[]{:S(2)}) copy-start(bf16[32,2,2048]{2,1,0:T(2,128)(2,1)} %param.14) | copy-start | bytes 786436
  356.8 67.1 %copy-start.12 = (f32[2048]{0:T(1024)S(1)}, f32[2048]{0:T(1024)}, u32[]{:S(2)}) copy-start(f32[2048]{0:T(1024)} %param.23) | copy-start | bytes 24580
  356.8 122.1 %all-gather.5.cloned.1.call-start = ((), (), s32[]{:S(2)}) async-start(), calls=%async_computation.4 | async-start | bytes 2359296 | tf_op jit(solution)/shard_map/all_gather | solution.py:112
  424.8 120.7 %reduce-scatter.5.cloned.1.call-start = ((), (), s32[]{:S(2)}) async-start(), calls=%async_computation.5 | async-start | bytes 2359296 | tf_op jit(solution)/shard_map/reduce_scatter | solution.py:118
  483.3 64.2 %copy-start.1 = (bf16[2048,3,256]{2,0,1:T(8,128)(2,1)S(1)}, bf16[2048,3,256]{2,0,1:T(8,128)(2,1)}, u32[]{:S(2)}) copy-start(bf16[2048,3,256]{2,0,1:T(8,128)(2,1)} %param.21) | copy-start | bytes 9437188
Sparse Core Ops, SparseCore 0:
  10.0 57.4 all-gather.2
  356.9 65.5 reduce-scatter.2
  424.9 53.9 all-gather.4
  491.2 54.2 reduce-scatter.4
Sparse Core Ops, SparseCore 1:
  14.9 312.1 all-reduce.2
where the time goes:
time: 556 us; the launch traced here: 555 us
  waiting for transfers between devices  471 us (85%)
  local copies, waits for them, and re-layouts  24 us (4%)
  other arithmetic  21.9 us (4%)
  matrix products  21 us (4%)
  between operations  16.1 us (3%)
    psum x1, waiting for transfers between devices, from_root(): return lax.psum(block, axis)  247 us
    reduce_scatter x1, waiting for transfers between devices, on_device(): lax.psum_scatter(jnp.einsum('srk,kd->srd', block, w_out_attn, preferred_e...  65.7 us
    reduce_scatter x1, waiting for transfers between devices, on_device(): lax.psum_scatter(jnp.einsum('srf,fd->srd', block, w_down, preferred_eleme...  54.3 us
    all_gather x1, waiting for transfers between devices, on_device(): lax.all_gather(normed, 'tp', axis=0, tiled=True)  54.1 us
    all_gather x1, waiting for transfers between devices, project_rows(): gathered = lax.all_gather(suffix, 'tp', axis=0, tiled=True)  49.8 us
  transfers between devices with their start and end apart: 5, of which 5 were waited for; matrix products, arithmetic and copies ran while one was open for 4% of the time, Pallas kernels for 0%

commit v1 on v0

v1 whole, which is shorter than its diff:
```python
import functools

import jax
import jax.numpy as jnp
from jax import lax
from jax.experimental import pallas as pl
from jax.experimental.pallas import tpu as pltpu
from jax.sharding import PartitionSpec as P

HD = 128
MESH = pl.DeviceIdType.MESH
F32 = jnp.float32
BF16 = jnp.bfloat16
VMEM_LIMIT = 60 * 1024 * 1024


class Place:
    def __init__(self):
        r, t = lax.axis_index("req"), lax.axis_index("tp")
        self.r, self.t = r, t
        self.core, self.y, self.zh = r % 2, (r // 2) % 4, r // 8
        self.x, self.zl = t // 2, t % 2
        self.mate = {"req": r + 1 - 2 * self.core}
        self.yp = {"req": self.zh * 8 + ((self.y + 1) % 4) * 2 + self.core}
        self.ym = {"req": self.zh * 8 + ((self.y + 3) % 4) * 2 + self.core}
        self.zp = {"req": ((self.zh + 1) % 4) * 8 + self.y * 2 + self.core}
        self.zm = {"req": ((self.zh + 3) % 4) * 8 + self.y * 2 + self.core}
        self.xp = {"tp": ((self.x + 1) % 4) * 2 + self.zl}
        self.xm = {"tp": ((self.x + 3) % 4) * 2 + self.zl}
        self.zz = {"tp": self.x * 2 + 1 - self.zl}


class Wire:
    def __init__(self, ssem, rsem):
        self.ssem, self.rsem, self.n, self.sent = ssem, rsem, 0, []

    def send(self, src, dst, to, into=None):
        k = self.n
        self.n += 1
        copy = pltpu.make_async_remote_copy(
            src_ref=src, dst_ref=dst, send_sem=self.ssem.at[k], recv_sem=self.rsem.at[k],
            device_id=to, device_id_type=MESH)
        copy.start()
        self.sent.append(copy)
        into = dst if into is None else into
        here = pltpu.make_async_remote_copy(
            src_ref=into, dst_ref=into, send_sem=self.ssem.at[k], recv_sem=self.rsem.at[k],
            device_id=to, device_id_type=MESH)
        return here.wait_recv

    def drain(self):
        for copy in self.sent:
            copy.wait_send()


def greet(peers):
    barrier = pltpu.get_barrier_semaphore()
    for peer in peers:
        pl.semaphore_signal(barrier, inc=1, device_id=peer, device_id_type=MESH)
    pl.semaphore_wait(barrier, len(peers))


def merge(streams):
    due = [next(s, None) for s in streams]
    while any(d is not None for d in due):
        i = min((d, k) for k, d in enumerate(due) if d is not None)[1]
        due[i] = next(streams[i], None)


def scatter_ring(wire, at, me, left, right, rooms, mix, final, times):
    rbr, rbl, fr, fl = rooms
    opp, nxt, prv = (me + 2) % 4, (me + 1) % 4, (me + 3) % 4
    w_rbr = wire.send(at(opp, 0), rbr, left)
    w_rbl = wire.send(at(opp, 1), rbl, right)
    w_fr1 = wire.send(at(prv, 1), fr.at[1], left)
    w_fl0 = wire.send(at(nxt, 0), fl.at[0], right)
    yield times[0]
    w_rbr()
    mix(at(prv, 0), rbr)
    w_fr0 = wire.send(at(prv, 0), fr.at[0], left)
    w_rbl()
    mix(at(nxt, 1), rbl)
    w_fl1 = wire.send(at(nxt, 1), fl.at[1], right)
    yield times[1]
    w_fr1()
    w_fl0()
    w_fr0()
    w_fl1()
    for j in range(2):
        final(j, at(me, j), fr.at[j], fl.at[j])


def gather_ring(wire, at, me, left, right, times, got=None):
    opp, nxt, prv = (me + 2) % 4, (me + 1) % 4, (me + 3) % 4
    w_r = wire.send(at(me, None), at(me, None), left, at(nxt, None))
    w_l = wire.send(at(me, None), at(me, None), right, at(prv, None))
    yield times[0]
    w_l()
    w_o0 = wire.send(at(prv, 0), at(prv, 0), right, at(opp, 0))
    if got:
        got(prv)
    w_r()
    w_o1 = wire.send(at(nxt, 1), at(nxt, 1), left, at(opp, 1))
    if got:
        got(nxt)
    yield times[1]
    w_o0()
    w_o1()
    if got:
        got(opp)


def rows_at(ref, base, size):
    def at(k, j):
        if j is None:
            return ref.at[pl.ds(pl.multiple_of(base + k * size, size), size)]
        half = size // 2
        return ref.at[pl.ds(pl.multiple_of(base + k * size + j * half, half), half)]

    return at


def normalize(values, gain):
    values = values.astype(F32)
    center = values - jnp.mean(values, -1, keepdims=True)
    spread = jnp.mean(center * center, -1, keepdims=True)
    return (center * lax.rsqrt(spread + 1e-05) * gain).astype(BF16)


def gather_z_first(wire, p, ref, times):
    own = ref.at[pl.ds(pl.multiple_of(p.t * 32, 32), 32)]
    w_z = wire.send(own, own, p.zz, ref.at[pl.ds(pl.multiple_of(p.x * 64 + (1 - p.zl) * 32, 32), 32)])

    def at(zl):
        def inner(k, j):
            if j is None:
                return ref.at[pl.ds(pl.multiple_of(k * 64 + zl * 32, 32), 32)]
            return ref.at[pl.ds(pl.multiple_of(k * 64 + zl * 32 + j * 16, 16), 16)]
        return inner

    mine = gather_ring(wire, at(p.zl), p.x, p.xm, p.xp, times[1:3])
    next(mine)
    yield times[0]
    w_z()
    other = gather_ring(wire, at(1 - p.zl), p.x, p.xm, p.xp, times[3:5])
    next(other)
    yield times[1]
    next(mine)
    yield times[2]
    next(mine, None)
    yield times[3]
    next(other)
    yield times[4]
    next(other, None)


def gather_x_first(wire, p, ref, times):
    def piece(k, zl):
        return ref.at[pl.ds(pl.multiple_of(k * 64 + zl * 32, 32), 32)]

    def at(k, j):
        if j is None:
            return piece(k, p.zl)
        return ref.at[pl.ds(pl.multiple_of(k * 64 + p.zl * 32 + j * 16, 16), 16)]

    waits = []

    def got(k):
        waits.append(wire.send(piece(k, p.zl), piece(k, p.zl), p.zz, piece(k, 1 - p.zl)))

    ring = gather_ring(wire, at, p.x, p.xm, p.xp, times[0:2], got)
    due = next(ring)
    got(p.x)
    while due is not None:
        yield due
        due = next(ring, None)
    yield times[2]
    for wait in waits:
        wait()


def prefix_half(wire, p, a, kv, own, par, rooms, owner, times):
    held = owner == p.r
    chip = owner // 2 == p.r // 2
    row = owner // 8 == p.zh
    con, done = own.at[a], kv.at[p.core, a]
    con[...] = jnp.where(held, own[a], par[a])
    yrooms, zrooms = rooms
    whose = {}

    def mix(ref, got):
        ref[...] = jnp.where(whose["own"], ref[...], got[...])

    def final(j, ref, fr, fl):
        d = (whose["at"] - whose["me"] + 4) % 4
        far = fr if j == 0 else fl
        near, near_d = (fl, 3) if j == 0 else (fr, 1)
        into = whose["into"](whose["me"], j)
        into[...] = jnp.where(d == 0, ref[...], jnp.where(d == near_d, near[...], far[...]))

    yat = rows_at(con, 0, 512)
    whose.update(own=chip, at=(owner // 2) % 4, me=p.y, into=yat)
    yield from scatter_ring(wire, yat, p.y, p.ym, p.yp, yrooms, mix, final, times[0:2])
    zat, zdone = rows_at(con, p.y * 512, 128), rows_at(done, p.y * 512, 128)
    ydone = rows_at(done, 0, 512)
    whose.update(own=row, at=owner // 8, me=p.zh, into=zdone)
    yield from scatter_ring(wire, zat, p.zh, p.zm, p.zp, zrooms, mix, final, times[2:4])
    yield from gather_ring(wire, zdone, p.zh, p.zm, p.zp, times[4:6])
    theirs = rows_at(kv.at[1 - p.core, a], 0, 512)
    waits = []

    def got(k):
        waits.append(wire.send(ydone(k, None), ydone(k, None), p.mate, theirs(k, None)))

    ring = gather_ring(wire, ydone, p.y, p.ym, p.yp, times[6:8], got)
    due = next(ring)
    got(p.y)
    while due is not None:
        yield due
        due = next(ring, None)
    yield times[8]
    for wait in waits:
        wait()


def attend(qkv, kv, ctx, s, group, length):
    scale = HD ** (-0.5)
    rows = lax.broadcasted_iota(jnp.int32, (256, 256), 0)
    cols = lax.broadcasted_iota(jnp.int32, (256, 256), 1)
    visible = (cols <= rows) & (cols < length)
    nt = (((1,), (1,)), ((), ()))
    for h in range(2):
        lanes = slice(h * HD, (h + 1) * HD)
        q = qkv[0, s, :, lanes]
        pre = lax.dot_general(q, kv[group, 0, :, lanes], nt, preferred_element_type=F32) * scale
        own = lax.dot_general(q, qkv[1, s, :, lanes], nt, preferred_element_type=F32) * scale
        own = jnp.where(visible, own, -jnp.inf)
        top = jnp.maximum(jnp.max(pre, -1, keepdims=True), jnp.max(own, -1, keepdims=True))
        pre = jnp.exp(pre - top)
        own = jnp.exp(own - top)
        total = jnp.sum(pre, -1, keepdims=True) + jnp.sum(own, -1, keepdims=True)
        out = jnp.dot(pre.astype(BF16), kv[group, 1, :, lanes], preferred_element_type=F32)
        out = out + jnp.dot(own.astype(BF16), qkv[2, s, :, lanes], preferred_element_type=F32)
        ctx[s, :, lanes] = (out / total).astype(BF16)


def first_kernel(owner_ref, group_ref, perm_ref, len_ref, x_ref, gain_ref, block, w_any, ctx,
                 xg, own, par, kv, w, qkv, yr0, yf0, yr1, yf1, zr0, zf0, zr1, zf1, ssem, rsem, lsem):
    p = Place()
    copies = [pltpu.make_async_copy(block.at[a], own.at[a], lsem.at[a]) for a in range(2)]
    weights = pltpu.make_async_copy(w_any, w, lsem.at[2])
    for copy in copies:
        copy.start()
    weights.start()
    greet([p.mate, p.yp, p.ym, p.zp, p.zm, p.xp, p.xm, p.zz])
    wire = Wire(ssem, rsem)
    w_par = [wire.send(block.at[a], par.at[a], p.mate) for a in range(2)]
    for s in range(2):
        xg[s, pl.ds(pl.multiple_of(p.t * 32, 32), 32)] = normalize(x_ref[s], gain_ref[...])
    owner = owner_ref[p.core]

    def prefix(a, start, times):
        yield start
        copies[a].wait()
        w_par[a]()
        yr, yf, zr, zf = ((yr0, yf0, zr0, zf0), (yr1, yf1, zr1, zf1))[a]
        rooms = ((yr.at[0], yr.at[1], yf.at[0], yf.at[1]), (zr.at[0], zr.at[1], zf.at[0], zf.at[1]))
        yield from prefix_half(wire, p, a, kv, own, par, rooms, owner, times)

    def project(start):
        yield start
        weights.wait()
        for s in (1, 0):
            @pl.loop(0, 3)
            def _(j):
                qkv[j, s] = jnp.dot(xg[s], w[j], preferred_element_type=F32).astype(BF16)
            yield start + 1

    merge([
        gather_z_first(wire, p, xg.at[0], (4, 9, 12, 15, 18)),
        gather_x_first(wire, p, xg.at[1], (5, 8, 20)),
        prefix(0, 2, (8, 12, 15, 18, 21, 24, 29, 33, 40)),
        prefix(1, 5, (15, 20, 24, 26, 29, 31, 38, 42, 46)),
        project(21),
    ])
    for s in range(2):
        request = perm_ref[p.r * 2 + s]
        attend(qkv, kv, ctx, s, group_ref[request], len_ref[request])
    wire.drain()


def add_rings(wire, p, part, rooms, times):
    pass


def gelu(v):
    return jax.nn.gelu(v, approximate=False)


def on_device(suffix, prefix_store, prefix_owner, prefix_group, request_perm, suffix_len, ln_gain_attn,
              w_qkv, w_out_attn, ln_gain_mlp, w_in, w_down):
    rows = jnp.transpose(suffix, (1, 0, 2))
    block = jnp.transpose(prefix_store[0], (1, 0, 2))
    w3 = jnp.transpose(w_qkv, (1, 0, 2))
    vm = pl.BlockSpec(memory_space=pltpu.VMEM)
    sm = pl.BlockSpec(memory_space=pltpu.SMEM)
    anym = pl.BlockSpec(memory_space=pl.ANY)
    context = pl.pallas_call(
        first_kernel,
        out_shape=jax.ShapeDtypeStruct((2, 256, 256), BF16),
        in_specs=[sm, sm, sm, sm, vm, vm, anym, anym],
        out_specs=vm,
        scratch_shapes=[
            pltpu.VMEM((2, 256, 2048), BF16),
            pltpu.VMEM((2, 2048, 256), BF16),
            pltpu.VMEM((2, 2048, 256), BF16),
            pltpu.VMEM((2, 2, 2048, 256), BF16),
            pltpu.VMEM((3, 2048, 256), BF16),
            pltpu.VMEM((3, 2, 256, 256), BF16),
            pltpu.VMEM((2, 256, 256), BF16),
            pltpu.VMEM((2, 2, 256, 256), BF16),
            pltpu.VMEM((2, 256, 256), BF16),
            pltpu.VMEM((2, 2, 256, 256), BF16),
            pltpu.VMEM((2, 64, 256), BF16),
            pltpu.VMEM((2, 2, 64, 256), BF16),
            pltpu.VMEM((2, 64, 256), BF16),
            pltpu.VMEM((2, 2, 64, 256), BF16),
            pltpu.SemaphoreType.DMA((96,)),
            pltpu.SemaphoreType.DMA((96,)),
            pltpu.SemaphoreType.DMA((4,)),
        ],
        compiler_params=pltpu.CompilerParams(
            collective_id=0, has_side_effects=True, vmem_limit_bytes=VMEM_LIMIT),
        name="gather_project_attend",
    )(prefix_owner, prefix_group, request_perm, suffix_len, rows, ln_gain_attn.reshape(1, -1), block, w3)
    context = jnp.transpose(context, (1, 0, 2))
    return rest(context, suffix, request_perm, suffix_len, w_out_attn, ln_gain_mlp, w_in, w_down)


def layer_norm(values, gain):
    values = values.astype(jnp.float32)
    center = values - jnp.mean(values, -1, keepdims=True)
    spread = jnp.mean(center * center, -1, keepdims=True)
    return center * lax.rsqrt(spread + 1e-05) * gain


def rest(context, suffix, request_perm, suffix_len, w_out_attn, ln_gain_mlp, w_in, w_down):
    part_rows, slots_dev, _ = suffix.shape
    slots = lax.axis_index("req") * slots_dev + jnp.arange(slots_dev, dtype=jnp.int32)
    lengths = jnp.take(suffix_len, jnp.take(request_perm, slots))
    first_row = lax.axis_index("tp") * part_rows
    attention = lax.psum_scatter(
        jnp.einsum("srk,kd->srd", context, w_out_attn, preferred_element_type=jnp.float32).astype(
            jnp.bfloat16), "tp", scatter_dimension=0, tiled=True).astype(jnp.float32)
    hidden = (suffix.astype(jnp.float32) + attention).astype(jnp.bfloat16)
    normed = layer_norm(hidden, ln_gain_mlp).astype(jnp.bfloat16)
    product = jnp.einsum("srd,df->srf", lax.all_gather(normed, "tp", axis=0, tiled=True), w_in,
                         preferred_element_type=jnp.float32)
    inner = jax.nn.gelu(product, approximate=False).astype(jnp.bfloat16)
    down = lax.psum_scatter(
        jnp.einsum("srf,fd->srd", inner, w_down, preferred_element_type=jnp.float32).astype(
            jnp.bfloat16), "tp", scatter_dimension=0, tiled=True).astype(jnp.float32)
    places = first_row + jnp.arange(part_rows, dtype=jnp.int32)
    valid = places[:, None] < lengths[None, :]
    return jnp.where(valid[:, :, None], hidden.astype(jnp.float32) + down, 0.0).astype(jnp.bfloat16)


def solution(mesh):
    placed = (P("tp", "req", None), P("req", None, None, "tp"), P(), P(), P(), P(), P(),
              P(None, None, "tp"), P("tp", None), P(), P(None, "tp"), P("tp", None))
    return jax.shard_map(
        on_device, mesh=mesh, in_specs=placed, out_specs=P("tp", "req", None), check_vma=False)
```

time: 556 us -> 275 us (0.49)
  waiting for transfers between devices: 471 us -> 162 us
  Pallas kernels: 0 us -> 74.5 us
  other arithmetic: 21.9 us -> 3.4 us
  local copies, waits for them, and re-layouts: 24 us -> 7.01 us
  matrix products: 21 us -> 13.1 us
    psum x1 -> x0, waiting for transfers between devices: 247 us -> none  [from_root(): return lax.psum(block, axis)]
    pallas_call x0 -> x1, Pallas kernels: none -> 74.5 us  [on_device(): pl.pallas_call(first_kernel, out_shape=jax.ShapeDtypeStruct((2, 256, 256)...]
    all_gather x2 -> x1, waiting for transfers between devices: 104 us -> 53.9 us  [rest(): lax.all_gather(normed, 'tp', axis=0, tiled=True)]
    reduce_scatter x2, waiting for transfers between devices: 120 us -> 108 us  [the longest x1 55.8 us: rest(): lax.psum_scatter(jnp.einsum('srk,kd->srd', context, w_out_attn, preferred...]
    slice x5 -> x0, local copies, waits for them, and re-layouts: 9.19 us -> none  [the longest x2 4.54 us: attend(): keys_pre = cached[:, :, 0].reshape(slots_dev, prefix_rows, heads, HD)]
    gather x6 -> x2, local copies, waits for them, and re-layouts: 9.98 us -> 1.27 us  [rest(): lengths = jnp.take(suffix_len, jnp.take(request_perm, slots))]
    dot_general x8 -> x3, matrix products: 21 us -> 13.1 us  [the longest x1 5.66 us: rest(): jnp.einsum('srf,fd->srd', inner, w_down, preferred_element_type=jnp.float32)]
    select_n x5 -> x3, other arithmetic: 6.83 us -> 0.03 us  [rest(): lengths = jnp.take(suffix_len, jnp.take(request_perm, slots))]
  transfers between devices with their start and end apart: 5 -> 3, of which waited for: 5 -> 3; matrix products, arithmetic and copies ran while one was open for 4% -> 1% of each run, Pallas kernels for 0% -> 0%
where the time goes in v1:
time: 275 us; the launch traced here: 274 us
  waiting for transfers between devices  162 us (59%)
  Pallas kernels  74.5 us (27%)
  between operations  13.2 us (5%)
  matrix products  13.1 us (5%)
  local copies, waits for them, and re-layouts  7.01 us (3%)
  other arithmetic  3.4 us (1%)
    pallas_call x1, Pallas kernels, on_device(): pl.pallas_call(first_kernel, out_shape=jax.ShapeDtypeStruct((2, 256, 256)...  74.5 us
    reduce_scatter x1, waiting for transfers between devices, rest(): lax.psum_scatter(jnp.einsum('srk,kd->srd', context, w_out_attn, preferred...  55.8 us
    all_gather x1, waiting for transfers between devices, rest(): lax.all_gather(normed, 'tp', axis=0, tiled=True)  53.9 us
    reduce_scatter x1, waiting for transfers between devices, rest(): lax.psum_scatter(jnp.einsum('srf,fd->srd', inner, w_down, preferred_eleme...  52.4 us
    dot_general x1, matrix products, rest(): jnp.einsum('srf,fd->srd', inner, w_down, preferred_element_type=jnp.float32)  5.66 us
  transfers between devices with their start and end apart: 3, of which 3 were waited for; matrix products, arithmetic and copies ran while one was open for 1% of the time, Pallas kernels for 0%

profile of v1, /device:TPU:16, one launch (start us, length us, event | category | flops | bytes accessed | tf_op | source)
XLA Modules:
  0.0 273.7 jit_solution(1597712801634008805)
XLA Ops:
  6.5 0.0 copy-start
  6.5 0.0 copy-start.4
  6.5 0.0 reduce-scatter.3.cloned.1.call-start
  6.5 3.4 %copy.25 = bf16[1,2048,2,256]{3,1,2,0:T(8,128)(2,1)} copy(bf16[1,2048,2,256]{3,2,1,0:T(2,128)(2,1)} %param.15) | data formatting | bytes 4194304 | tf_op args[1]
  9.9 0.0 copy-done.4
  9.9 0.8 copy.26
  10.7 0.0 copy-start.3
  10.7 74.5 %gather_project_attend.1 = bf16[2,256,256]{2,1,0:T(8,128)(2,1)} custom-call(s32[2]{0:T(128)} %owner_ref.1, s32[64]{0:T(128)} %group_ref.1, s32[64]{0:T(128)} %perm_ref.1, s32[64]{0:T(128)} %len_ref.1, bf16[2,32,2048]{2,1,0:T(8,128)(2,1)} %bitcast.27, f32[1,2048]{1,0:T(1,128)} %bitcast.28, bf16[2,2048,256]{2,1,0:T(8,128)(2,1)} %bitcast.25, ...), custom_call_target="tpu_custom_call" | custom-call | tf_op jit(solution)/shard_map/gather_project_attend/pallas_call | solution.py:308
  85.3 0.0 copy-done.3
  85.3 3.0 %convolution_convert_fusion = bf16[256,2,2048]{2,0,1:T(8,128)(2,1)} fusion(bf16[256,2048]{1,0:T(8,128)(2,1)S(1)} %copy-done.3, bf16[2,256,256]{2,1,0:T(8,128)(2,1)} %gather_project_attend.1), kind=kOutput, calls=%fused_computation.2 | convolution fusion | flops 537919488 | bytes 3407872 | tf_op jit(solution)/shard_map/srk,kd->srd/dot_general | solution.py:353
  88.3 0.0 copy-start.5
  88.3 0.0 copy-start.6
  88.3 0.0 reduce-scatter.3.cloned.1.call-update
  88.3 0.0 all-gather.2.cloned.1.call-start
  88.4 55.8 %reduce-scatter.3.cloned.1.call-done = bf16[32,2,2048]{2,0,1:T(8,128)(2,1)} async-done(((bf16[256,2,2048]{2,0,1:T(8,128)(2,1)}), bf16[32,2,2048]{2,0,1:T(8,128)(2,1)}) %reduce-scatter.3.cloned.1.call-update) | async-done | bytes 262160 | tf_op jit(solution)/shard_map/reduce_scatter | solution.py:352
  144.2 0.0 copy-done.5
  144.2 1.1 convert_reduce_fusion
  145.3 0.2 fusion.47
  145.6 0.0 copy-done.6
  145.6 0.9 fusion.49
  146.4 0.0 all-gather.2.cloned.1.call-update
  146.5 0.2 reduce-scatter.5.cloned.1.call-start
  146.7 53.9 %all-gather.2.cloned.1.call-done = bf16[256,2,2048]{2,0,1:T(8,128)(2,1)} async-done(((bf16[32,2,2048]{2,0,1:T(8,128)(2,1)}), bf16[256,2,2048]{2,0,1:T(8,128)(2,1)}) %all-gather.2.cloned.1.call-update) | async-done | bytes 2097168 | tf_op jit(solution)/shard_map/all_gather | solution.py:357
  200.6 4.4 %fusion.53 = (u8[256,640]{1,0:T(8,128)(4,1)S(1)}, u8[256,640]{1,0:T(8,128)(4,1)S(1)}, f32[256,2,640]{2,0,1:T(8,128)S(1)}) fusion(bf16[256,2,2048]{2,0,1:T(8,128)(2,1)} %all-gather.2.cloned.1.call-done, bf16[2048,640]{1,0:T(8,128)(2,1)} %param.24), kind=kOutput, calls=%fused_computation.74 | convolution fusion | flops 1346109440 | bytes 6356992 | tf_op jit(solution)/shard_map/srd,df->srf/dot_general | solution.py:357
  205.0 0.0 copy-done
  205.0 5.7 %convolution_convert_fusion.1 = bf16[256,2,2048]{2,0,1:T(8,128)(2,1)} fusion(bf16[640,2048]{1,0:T(8,128)(2,1)S(1)} %copy-done, f32[256,2,640]{2,0,1:T(8,128)S(1)} %get-tuple-element.10, u8[256,640]{1,0:T(8,128)(4,1)S(1)} %get-tuple-element.7, u8[256,640]{1,0:T(8,128)(4,1)S(1)} %get-tuple-element.6), kind=kOutput, calls=%fused_computation.3 | convolution fusion | flops 1366163456 | bytes 6356992 | tf_op jit(solution)/shard_map/srf,fd->srd/dot_general | solution.py:361
  210.7 0.0 copy-start.1
  210.7 0.0 copy-start.2
  210.7 0.0 reduce-scatter.5.cloned.1.call-update
  210.7 0.6 copy-done.1
  211.3 0.6 gather_fusion
  212.0 0.0 copy-done.2
  212.0 0.6 gather_fusion.1
  212.7 0.1 broadcast_compare_fusion
  212.7 52.4 %reduce-scatter.5.cloned.1.call-done = bf16[32,2,2048]{2,0,1:T(8,128)(2,1)} async-done(((bf16[256,2,2048]{2,0,1:T(8,128)(2,1)}), bf16[32,2,2048]{2,0,1:T(8,128)(2,1)}) %reduce-scatter.5.cloned.1.call-update) | async-done | bytes 262160 | tf_op jit(solution)/shard_map/reduce_scatter | solution.py:360
  265.2 1.0 fusion.51
  266.2 1.0 copy.20
  (8 shorter events, 0.1 us)
Async XLA Ops:
  6.5 198.5 %copy-start = (bf16[640,2048]{1,0:T(8,128)(2,1)S(1)}, bf16[640,2048]{1,0:T(8,128)(2,1)}, u32[]{:S(2)}) copy-start(bf16[640,2048]{1,0:T(8,128)(2,1)} %param.25) | copy-start | bytes 7864324
  6.5 3.4 %copy-start.4 = (bf16[32,2,2048]{2,1,0:T(2,128)(2,1)S(1)}, bf16[32,2,2048]{2,1,0:T(2,128)(2,1)}, u32[]{:S(2)}) copy-start(bf16[32,2,2048]{2,1,0:T(2,128)(2,1)} %param.14) | copy-start | bytes 786436
  6.5 137.7 %reduce-scatter.3.cloned.1.call-start = ((), (), s32[]{:S(2)}) async-start(), calls=%async_computation.2 | async-start | bytes 2359296 | tf_op jit(solution)/shard_map/reduce_scatter | solution.py:352
  10.7 74.6 %copy-start.3 = (bf16[256,2048]{1,0:T(8,128)(2,1)S(1)}, bf16[256,2048]{1,0:T(8,128)(2,1)}, u32[]{:S(2)}) copy-start(bf16[256,2048]{1,0:T(8,128)(2,1)} %param.22) | copy-start | bytes 3145732
  88.3 55.9 %copy-start.5 = (bf16[32,2,2048]{2,1,0:T(2,128)(2,1)S(1)}, bf16[32,2,2048]{2,1,0:T(2,128)(2,1)}, u32[]{:S(2)}) copy-start(bf16[32,2,2048]{2,1,0:T(2,128)(2,1)} %param.14) | copy-start | bytes 786436
  88.3 57.3 %copy-start.6 = (f32[2048]{0:T(1024)S(1)}, f32[2048]{0:T(1024)}, u32[]{:S(2)}) copy-start(f32[2048]{0:T(1024)} %param.23) | copy-start | bytes 24580
  88.3 112.3 %all-gather.2.cloned.1.call-start = ((), (), s32[]{:S(2)}) async-start(), calls=%async_computation.3 | async-start | bytes 2359296 | tf_op jit(solution)/shard_map/all_gather | solution.py:357
  146.5 118.7 %reduce-scatter.5.cloned.1.call-start = ((), (), s32[]{:S(2)}) async-start(), calls=%async_computation.4 | async-start | bytes 2359296 | tf_op jit(solution)/shard_map/reduce_scatter | solution.py:360
  210.7 0.7 copy-start.1
  210.7 1.3 copy-start.2
Sparse Core Ops, SparseCore 0:
  88.4 55.7 reduce-scatter.2
  146.6 53.9 all-gather.1
  210.8 54.2 reduce-scatter.4

commit v2 on v1

--- a/solution.py
+++ b/solution.py
@@ -1,5 +1,3 @@
-import functools
-
 import jax
 import jax.numpy as jnp
 from jax import lax
@@ -244,14 +242,77 @@
         ctx[s, :, lanes] = (out / total).astype(BF16)
 
 
-def first_kernel(owner_ref, group_ref, perm_ref, len_ref, x_ref, gain_ref, block, w_any, ctx,
-                 xg, own, par, kv, w, qkv, yr0, yf0, yr1, yf1, zr0, zf0, zr1, zf1, ssem, rsem, lsem):
+def add(ref, got):
+    ref[...] = (ref[...].astype(F32) + got[...].astype(F32)).astype(BF16)
+
+
+def scatter_z_first(wire, p, part, total, away, zroom, rooms, times):
+    order = [(p.x + d) % 4 for d in (2, 3, 1, 0)]
+
+    def rows(k, zl):
+        return part.at[pl.ds(pl.multiple_of(k * 64 + zl * 32, 32), 32)]
+
+    def at(k, j):
+        return part.at[pl.ds(pl.multiple_of(k * 64 + p.zl * 32 + j * 16, 16), 16)]
+
+    def final(j, ref, fr, fl):
+        total[j * 16:(j + 1) * 16] = ref[...].astype(F32) + fr[...].astype(F32) + fl[...].astype(F32)
+
+    waits = [wire.send(rows(k, 1 - p.zl), zroom.at[i], p.zz) for i, k in enumerate(order)]
+    yield times[0]
+    for i in range(3):
+        waits[i]()
+        add(rows(order[i], p.zl), zroom.at[i])
+    yield from scatter_ring(wire, at, p.x, p.xm, p.xp, rooms, add, final, times[1:3])
+    waits[3]()
+    total[...] = total[...] + zroom[3].astype(F32)
+
+
+def scatter_x_first(wire, p, part, total, away, zroom, rooms, times):
+    waits = []
+
+    def at(k, j):
+        zl = p.zl if j else 1 - p.zl
+        return part.at[pl.ds(pl.multiple_of(k * 64 + zl * 32, 32), 32)]
+
+    def final(j, ref, fr, fl):
+        here = ref[...].astype(F32) + fr[...].astype(F32) + fl[...].astype(F32)
+        if j:
+            total[...] = here
+        else:
+            away[...] = here.astype(BF16)
+            waits.append(wire.send(away, zroom, p.zz))
+
+    yield from scatter_ring(wire, at, p.x, p.xm, p.xp, rooms, add, final, times[0:2])
+    yield times[2]
+    waits[0]()
+    total[...] = total[...] + zroom[...].astype(F32)
+
+
+def gelu(v):
+    return 0.5 * v * (1.0 + lax.erf(v * (0.5 ** 0.5)))
+
+
+def spread(left, w, into):
+    @pl.loop(0, 4)
+    def _(j):
+        lanes = pl.ds(pl.multiple_of(j * 512, 512), 512)
+        into[:, lanes] = jnp.dot(left[...], w[:, lanes], preferred_element_type=F32).astype(BF16)
+
+
+def layer_kernel(owner_ref, group_ref, perm_ref, len_ref, x_ref, gain_ref, gain2_ref, block, w_any, wo_any, wi_any,
+                 wd_any, out, xg, own, par, kv, w, qkv, yr0, yf0, yr1, yf1, zr0, zf0, zr1, zf1, ctx, wo, wi, wd,
+                 parts, total, hid, ng, inner, away, zra, zrb, xra, xfa, xrb, xfb, ssem, rsem, lsem):
     p = Place()
     copies = [pltpu.make_async_copy(block.at[a], own.at[a], lsem.at[a]) for a in range(2)]
     weights = pltpu.make_async_copy(w_any, w, lsem.at[2])
     for copy in copies:
         copy.start()
     weights.start()
+    later = [pltpu.make_async_copy(a, b, lsem.at[3 + i])
+             for i, (a, b) in enumerate([(wo_any, wo), (wi_any, wi), (wd_any, wd)])]
+    for copy in later:
+        copy.start()
     greet([p.mate, p.yp, p.ym, p.zp, p.zm, p.xp, p.xm, p.zz])
     wire = Wire(ssem, rsem)
     w_par = [wire.send(block.at[a], par.at[a], p.mate) for a in range(2)]
@@ -283,18 +344,44 @@
         prefix(1, 5, (15, 20, 24, 26, 29, 31, 38, 42, 46)),
         project(21),
     ])
-    for s in range(2):
-        request = perm_ref[p.r * 2 + s]
-        attend(qkv, kv, ctx, s, group_ref[request], len_ref[request])
+    requests = [perm_ref[p.r * 2 + s] for s in range(2)]
+
+    def scatter(s, step, times):
+        if s == 0:
+            rooms = (xra.at[step, 0], xra.at[step, 1], xfa.at[step, 0], xfa.at[step, 1])
+            return scatter_z_first(wire, p, parts.at[step, s], total.at[s], None, zra.at[step], rooms, times)
+        rooms = (xrb.at[step, 0], xrb.at[step, 1], xfb.at[step, 0], xfb.at[step, 1])
+        return scatter_x_first(wire, p, parts.at[step, s], total.at[s], away.at[step], zrb.at[step], rooms, times)
+
+    def slot(s, start, times):
+        yield start
+        attend(qkv, kv, ctx, s, group_ref[requests[s]], len_ref[requests[s]])
+        if s == 0:
+            later[0].wait()
+        spread(ctx.at[s], wo, parts.at[0, s])
+        yield from scatter(s, 0, times[0])
+        hid[s] = (x_ref[s].astype(F32) + total[s]).astype(BF16)
+        ng[s, pl.ds(pl.multiple_of(p.t * 32, 32), 32)] = normalize(hid[s], gain2_ref[...])
+        yield from (gather_x_first if s else gather_z_first)(wire, p, ng.at[s], times[1])
+        if s == 0:
+            later[1].wait()
+            later[2].wait()
+
+        @pl.loop(0, 2)
+        def _(i):
+            rows = pl.ds(pl.multiple_of(i * 128, 128), 128)
+            inner[s, rows] = gelu(jnp.dot(ng[s, rows], wi[...], preferred_element_type=F32)).astype(BF16)
+
+        spread(inner.at[s], wd, parts.at[1, s])
+        yield from scatter(s, 1, times[2])
+        places = p.t * 32 + lax.broadcasted_iota(jnp.int32, (32, 2048), 0)
+        out[s] = jnp.where(places < len_ref[requests[s]], hid[s].astype(F32) + total[s], 0.0).astype(BF16)
+
+    merge([
+        slot(0, 0, ((13, 16, 18.5), (23, 28, 31, 33, 35), (49, 52, 54.5))),
+        slot(1, 4, ((8.5, 13.5, 17.5), (22, 25, 37), (43, 48, 52.5))),
+    ])
     wire.drain()
-
-
-def add_rings(wire, p, part, rooms, times):
-    pass
-
-
-def gelu(v):
-    return jax.nn.gelu(v, approximate=False)
 
 
 def on_device(suffix, prefix_store, prefix_owner, prefix_group, request_perm, suffix_len, ln_gain_attn,
@@ -305,10 +392,10 @@
     vm = pl.BlockSpec(memory_space=pltpu.VMEM)
     sm = pl.BlockSpec(memory_space=pltpu.SMEM)
     anym = pl.BlockSpec(memory_space=pl.ANY)
-    context = pl.pallas_call(
-        first_kernel,
-        out_shape=jax.ShapeDtypeStruct((2, 256, 256), BF16),
-        in_specs=[sm, sm, sm, sm, vm, vm, anym, anym],
+    out = pl.pallas_call(
+        layer_kernel,
+        out_shape=jax.ShapeDtypeStruct((2, 32, 2048), BF16),
+        in_specs=[sm, sm, sm, sm, vm, vm, vm, anym, anym, anym, anym, anym],
         out_specs=vm,
         scratch_shapes=[
             pltpu.VMEM((2, 256, 2048), BF16),
@@ -325,44 +412,32 @@
             pltpu.VMEM((2, 2, 64, 256), BF16),
             pltpu.VMEM((2, 64, 256), BF16),
             pltpu.VMEM((2, 2, 64, 256), BF16),
-            pltpu.SemaphoreType.DMA((96,)),
-            pltpu.SemaphoreType.DMA((96,)),
-            pltpu.SemaphoreType.DMA((4,)),
+            pltpu.VMEM((2, 256, 256), BF16),
+            pltpu.VMEM((256, 2048), BF16),
+            pltpu.VMEM((2048, 640), BF16),
+            pltpu.VMEM((640, 2048), BF16),
+            pltpu.VMEM((2, 2, 256, 2048), BF16),
+            pltpu.VMEM((2, 32, 2048), F32),
+            pltpu.VMEM((2, 32, 2048), BF16),
+            pltpu.VMEM((2, 256, 2048), BF16),
+            pltpu.VMEM((2, 256, 640), BF16),
+            pltpu.VMEM((2, 32, 2048), BF16),
+            pltpu.VMEM((2, 4, 32, 2048), BF16),
+            pltpu.VMEM((2, 32, 2048), BF16),
+            pltpu.VMEM((2, 2, 16, 2048), BF16),
+            pltpu.VMEM((2, 2, 2, 16, 2048), BF16),
+            pltpu.VMEM((2, 2, 32, 2048), BF16),
+            pltpu.VMEM((2, 2, 2, 32, 2048), BF16),
+            pltpu.SemaphoreType.DMA((128,)),
+            pltpu.SemaphoreType.DMA((128,)),
+            pltpu.SemaphoreType.DMA((6,)),
         ],
         compiler_params=pltpu.CompilerParams(
             collective_id=0, has_side_effects=True, vmem_limit_bytes=VMEM_LIMIT),
-        name="gather_project_attend",
-    )(prefix_owner, prefix_group, request_perm, suffix_len, rows, ln_gain_attn.reshape(1, -1), block, w3)
-    context = jnp.transpose(context, (1, 0, 2))
-    return rest(context, suffix, request_perm, suffix_len, w_out_attn, ln_gain_mlp, w_in, w_down)
-
-
-def layer_norm(values, gain):
-    values = values.astype(jnp.float32)
-    center = values - jnp.mean(values, -1, keepdims=True)
-    spread = jnp.mean(center * center, -1, keepdims=True)
-    return center * lax.rsqrt(spread + 1e-05) * gain
-
-
-def rest(context, suffix, request_perm, suffix_len, w_out_attn, ln_gain_mlp, w_in, w_down):
-    part_rows, slots_dev, _ = suffix.shape
-    slots = lax.axis_index("req") * slots_dev + jnp.arange(slots_dev, dtype=jnp.int32)
-    lengths = jnp.take(suffix_len, jnp.take(request_perm, slots))
-    first_row = lax.axis_index("tp") * part_rows
-    attention = lax.psum_scatter(
-        jnp.einsum("srk,kd->srd", context, w_out_attn, preferred_element_type=jnp.float32).astype(
-            jnp.bfloat16), "tp", scatter_dimension=0, tiled=True).astype(jnp.float32)
-    hidden = (suffix.astype(jnp.float32) + attention).astype(jnp.bfloat16)
-    normed = layer_norm(hidden, ln_gain_mlp).astype(jnp.bfloat16)
-    product = jnp.einsum("srd,df->srf", lax.all_gather(normed, "tp", axis=0, tiled=True), w_in,
-                         preferred_element_type=jnp.float32)
-    inner = jax.nn.gelu(product, approximate=False).astype(jnp.bfloat16)
-    down = lax.psum_scatter(
-        jnp.einsum("srf,fd->srd", inner, w_down, preferred_element_type=jnp.float32).astype(
-            jnp.bfloat16), "tp", scatter_dimension=0, tiled=True).astype(jnp.float32)
-    places = first_row + jnp.arange(part_rows, dtype=jnp.int32)
-    valid = places[:, None] < lengths[None, :]
-    return jnp.where(valid[:, :, None], hidden.astype(jnp.float32) + down, 0.0).astype(jnp.bfloat16)
+        name="decoder_layer",
+    )(prefix_owner, prefix_group, request_perm, suffix_len, rows, ln_gain_attn.reshape(1, -1),
+      ln_gain_mlp.reshape(1, -1), block, w3, w_out_attn, w_in, w_down)
+    return jnp.transpose(out, (1, 0, 2))
 
 
 def solution(mesh):

time: 275 us -> 146 us (0.53)
  waiting for transfers between devices: 162 us -> 0 us
  Pallas kernels: 74.5 us -> 139 us
  between operations: 13.2 us -> 0.01 us
  matrix products: 13.1 us -> 0 us
  other arithmetic: 3.4 us -> 0 us
    reduce_scatter x2 -> x0, waiting for transfers between devices: 108 us -> none  [the longest x1 55.8 us: rest(): lax.psum_scatter(jnp.einsum('srk,kd->srd', context, w_out_attn, preferred...]
    pallas_call x1, Pallas kernels: 74.5 us -> 139 us  [on_device(): pl.pallas_call(layer_kernel, out_shape=jax.ShapeDtypeStruct((2, 32, 2048)...]
    all_gather x1 -> x0, waiting for transfers between devices: 53.9 us -> none  [rest(): lax.all_gather(normed, 'tp', axis=0, tiled=True)]
    dot_general x3 -> x0, matrix products: 13.1 us -> none  [the longest x1 5.66 us: rest(): jnp.einsum('srf,fd->srd', inner, w_down, preferred_element_type=jnp.float32)]
  transfers between devices with their start and end apart: 3 -> 0, of which waited for: 3 -> 0; matrix products, arithmetic and copies ran while one was open for 1% -> 0% of each run, Pallas kernels for 0% -> 0%
where the time goes in v2:
time: 146 us
  Pallas kernels  139 us (95%)
  local copies, waits for them, and re-layouts  6.87 us (5%)
    pallas_call x1, Pallas kernels, on_device(): pl.pallas_call(layer_kernel, out_shape=jax.ShapeDtypeStruct((2, 32, 2048)...  139 us
    unnamed x2, local copies, waits for them, and re-layouts  4.95 us

profile of v2, /device:TPU:16, one launch (start us, length us, event | category | flops | bytes accessed | tf_op | source)
XLA Modules:
  0.0 145.8 jit_solution(8896130395978732224)
XLA Ops:
  0.0 1.7 %copy.19 = bf16[32,2,2048]{2,0,1:T(8,128)(2,1)} copy(bf16[32,2,2048]{2,1,0:T(2,128)(2,1)} %param.12) | data formatting | bytes 524288 | tf_op args[0]
  1.7 3.2 %copy.18 = bf16[1,2048,2,256]{3,1,2,0:T(8,128)(2,1)} copy(bf16[1,2048,2,256]{3,2,1,0:T(2,128)(2,1)} %param.13) | data formatting | bytes 4194304 | tf_op args[1]
  4.9 138.9 %decoder_layer.1 = bf16[2,32,2048]{2,1,0:T(8,128)(2,1)} custom-call(s32[2]{0:T(128)} %owner_ref.1, s32[64]{0:T(128)} %group_ref.1, s32[64]{0:T(128)} %perm_ref.1, s32[64]{0:T(128)} %len_ref.1, bf16[2,32,2048]{2,1,0:T(8,128)(2,1)} %bitcast.15, f32[1,2048]{1,0:T(1,128)} %bitcast.16, f32[1,2048]{1,0:T(1,128)} %bitcast.17, bf16[2,2048,256]{2,1,0:T(8,128)(2,1)} %bitcast.12, ...), custom_call_target="tpu_custom_call" | custom-call | tf_op jit(solution)/shard_map/decoder_layer/pallas_call | solution.py:395
  143.9 1.9 %copy.15 = bf16[32,2,2048]{2,1,0:T(2,128)(2,1)} copy(bf16[32,2,2048]{2,0,1:T(8,128)(2,1)} %bitcast.14) | data formatting | bytes 524288 | tf_op jit(solution)/shard_map/transpose | solution.py:440

commit v3 on v2

--- a/solution.py
+++ b/solution.py
@@ -181,7 +181,7 @@
     held = owner == p.r
     chip = owner // 2 == p.r // 2
     row = owner // 8 == p.zh
-    con, done = own.at[a], kv.at[p.core, a]
+    con, done = own.at[a], kv[a].at[p.core]
     con[...] = jnp.where(held, own[a], par[a])
     yrooms, zrooms = rooms
     whose = {}
@@ -204,7 +204,7 @@
     whose.update(own=row, at=owner // 8, me=p.zh, into=zdone)
     yield from scatter_ring(wire, zat, p.zh, p.zm, p.zp, zrooms, mix, final, times[2:4])
     yield from gather_ring(wire, zdone, p.zh, p.zm, p.zp, times[4:6])
-    theirs = rows_at(kv.at[1 - p.core, a], 0, 512)
+    theirs = rows_at(kv[a].at[1 - p.core], 0, 512)
     waits = []
 
     def got(k):
@@ -221,25 +221,31 @@
         wait()
 
 
-def attend(qkv, kv, ctx, s, group, length):
+def weigh(qkv, keys, probs, own_probs, total, s, h, group, length):
     scale = HD ** (-0.5)
     rows = lax.broadcasted_iota(jnp.int32, (256, 256), 0)
     cols = lax.broadcasted_iota(jnp.int32, (256, 256), 1)
     visible = (cols <= rows) & (cols < length)
     nt = (((1,), (1,)), ((), ()))
+    lanes = slice(h * HD, (h + 1) * HD)
+    q = qkv[0, s, :, lanes]
+    pre = lax.dot_general(q, keys[group, :, lanes], nt, preferred_element_type=F32) * scale
+    own = lax.dot_general(q, qkv[1, s, :, lanes], nt, preferred_element_type=F32) * scale
+    own = jnp.where(visible, own, -jnp.inf)
+    top = jnp.maximum(jnp.max(pre, -1, keepdims=True), jnp.max(own, -1, keepdims=True))
+    pre = jnp.exp(pre - top)
+    own = jnp.exp(own - top)
+    total[s, h] = jnp.sum(pre, -1, keepdims=True) + jnp.sum(own, -1, keepdims=True)
+    probs[s, h] = pre.astype(BF16)
+    own_probs[s, h] = own.astype(BF16)
+
+
+def collect(qkv, values, probs, own_probs, total, ctx, s, group):
     for h in range(2):
         lanes = slice(h * HD, (h + 1) * HD)
-        q = qkv[0, s, :, lanes]
-        pre = lax.dot_general(q, kv[group, 0, :, lanes], nt, preferred_element_type=F32) * scale
-        own = lax.dot_general(q, qkv[1, s, :, lanes], nt, preferred_element_type=F32) * scale
-        own = jnp.where(visible, own, -jnp.inf)
-        top = jnp.maximum(jnp.max(pre, -1, keepdims=True), jnp.max(own, -1, keepdims=True))
-        pre = jnp.exp(pre - top)
-        own = jnp.exp(own - top)
-        total = jnp.sum(pre, -1, keepdims=True) + jnp.sum(own, -1, keepdims=True)
-        out = jnp.dot(pre.astype(BF16), kv[group, 1, :, lanes], preferred_element_type=F32)
-        out = out + jnp.dot(own.astype(BF16), qkv[2, s, :, lanes], preferred_element_type=F32)
-        ctx[s, :, lanes] = (out / total).astype(BF16)
+        out = jnp.dot(probs[s, h], values[group, :, lanes], preferred_element_type=F32)
+        out = out + jnp.dot(own_probs[s, h], qkv[2, s, :, lanes], preferred_element_type=F32)
+        ctx[s, :, lanes] = (out / total[s, h]).astype(BF16)
 
 
 def add(ref, got):
@@ -301,8 +307,9 @@
 
 
 def layer_kernel(owner_ref, group_ref, perm_ref, len_ref, x_ref, gain_ref, gain2_ref, block, w_any, wo_any, wi_any,
-                 wd_any, out, xg, own, par, kv, w, qkv, yr0, yf0, yr1, yf1, zr0, zf0, zr1, zf1, ctx, wo, wi, wd,
-                 parts, total, hid, ng, inner, away, zra, zrb, xra, xfa, xrb, xfb, ssem, rsem, lsem):
+                 wd_any, out, xg, own, par, keys, values, w, qkv, yr0, yf0, yr1, yf1, zr0, zf0, zr1, zf1, ctx, wo, wi, wd,
+                 parts, total, hid, ng, inner, away, zra, zrb, xra, xfa, xrb, xfb, probs, own_probs, weight,
+                 ssem, rsem, lsem):
     p = Place()
     copies = [pltpu.make_async_copy(block.at[a], own.at[a], lsem.at[a]) for a in range(2)]
     weights = pltpu.make_async_copy(w_any, w, lsem.at[2])
@@ -317,7 +324,7 @@
     wire = Wire(ssem, rsem)
     w_par = [wire.send(block.at[a], par.at[a], p.mate) for a in range(2)]
     for s in range(2):
-        xg[s, pl.ds(pl.multiple_of(p.t * 32, 32), 32)] = normalize(x_ref[s], gain_ref[...])
+        xg[s, pl.ds(pl.multiple_of(p.t * 32, 32), 32)] = normalize(x_ref[:, s, :], gain_ref[...])
     owner = owner_ref[p.core]
 
     def prefix(a, start, times):
@@ -326,7 +333,7 @@
         w_par[a]()
         yr, yf, zr, zf = ((yr0, yf0, zr0, zf0), (yr1, yf1, zr1, zf1))[a]
         rooms = ((yr.at[0], yr.at[1], yf.at[0], yf.at[1]), (zr.at[0], zr.at[1], zf.at[0], zf.at[1]))
-        yield from prefix_half(wire, p, a, kv, own, par, rooms, owner, times)
+        yield from prefix_half(wire, p, a, (keys, values), own, par, rooms, owner, times)
 
     def project(start):
         yield start
@@ -337,15 +344,22 @@
                 qkv[j, s] = jnp.dot(xg[s], w[j], preferred_element_type=F32).astype(BF16)
             yield start + 1
 
+    requests = [perm_ref[p.r * 2 + s] for s in range(2)]
+
+    def score(times):
+        for s in range(2):
+            for h in range(2):
+                yield times[2 * s + h]
+                weigh(qkv, keys, probs, own_probs, weight, s, h, group_ref[requests[s]], len_ref[requests[s]])
+
     merge([
         gather_z_first(wire, p, xg.at[0], (4, 9, 12, 15, 18)),
         gather_x_first(wire, p, xg.at[1], (5, 8, 20)),
         prefix(0, 2, (8, 12, 15, 18, 21, 24, 29, 33, 40)),
         prefix(1, 5, (15, 20, 24, 26, 29, 31, 38, 42, 46)),
         project(21),
+        score((40.5, 41.5, 42.5, 43.5)),
     ])
-    requests = [perm_ref[p.r * 2 + s] for s in range(2)]
-
     def scatter(s, step, times):
         if s == 0:
             rooms = (xra.at[step, 0], xra.at[step, 1], xfa.at[step, 0], xfa.at[step, 1])
@@ -355,12 +369,12 @@
 
     def slot(s, start, times):
         yield start
-        attend(qkv, kv, ctx, s, group_ref[requests[s]], len_ref[requests[s]])
+        collect(qkv, values, probs, own_probs, weight, ctx, s, group_ref[requests[s]])
         if s == 0:
             later[0].wait()
         spread(ctx.at[s], wo, parts.at[0, s])
         yield from scatter(s, 0, times[0])
-        hid[s] = (x_ref[s].astype(F32) + total[s]).astype(BF16)
+        hid[s] = (x_ref[:, s, :].astype(F32) + total[s]).astype(BF16)
         ng[s, pl.ds(pl.multiple_of(p.t * 32, 32), 32)] = normalize(hid[s], gain2_ref[...])
         yield from (gather_x_first if s else gather_z_first)(wire, p, ng.at[s], times[1])
         if s == 0:
@@ -379,14 +393,13 @@
 
     merge([
         slot(0, 0, ((13, 16, 18.5), (23, 28, 31, 33, 35), (49, 52, 54.5))),
-        slot(1, 4, ((8.5, 13.5, 17.5), (22, 25, 37), (43, 48, 52.5))),
+        slot(1, 2, ((7, 12, 16.5), (22, 25, 37), (43, 48, 52.5))),
     ])
     wire.drain()
 
 
 def on_device(suffix, prefix_store, prefix_owner, prefix_group, request_perm, suffix_len, ln_gain_attn,
               w_qkv, w_out_attn, ln_gain_mlp, w_in, w_down):
-    rows = jnp.transpose(suffix, (1, 0, 2))
     block = jnp.transpose(prefix_store[0], (1, 0, 2))
     w3 = jnp.transpose(w_qkv, (1, 0, 2))
     vm = pl.BlockSpec(memory_space=pltpu.VMEM)
@@ -401,7 +414,8 @@
             pltpu.VMEM((2, 256, 2048), BF16),
             pltpu.VMEM((2, 2048, 256), BF16),
             pltpu.VMEM((2, 2048, 256), BF16),
-            pltpu.VMEM((2, 2, 2048, 256), BF16),
+            pltpu.VMEM((2, 2048, 256), BF16),
+            pltpu.VMEM((2, 2048, 256), BF16),
             pltpu.VMEM((3, 2048, 256), BF16),
             pltpu.VMEM((3, 2, 256, 256), BF16),
             pltpu.VMEM((2, 256, 256), BF16),
@@ -428,6 +442,9 @@
             pltpu.VMEM((2, 2, 2, 16, 2048), BF16),
             pltpu.VMEM((2, 2, 32, 2048), BF16),
             pltpu.VMEM((2, 2, 2, 32, 2048), BF16),
+            pltpu.VMEM((2, 2, 256, 2048), BF16),
+            pltpu.VMEM((2, 2, 256, 256), BF16),
+            pltpu.VMEM((2, 2, 256, 1), F32),
             pltpu.SemaphoreType.DMA((128,)),
             pltpu.SemaphoreType.DMA((128,)),
             pltpu.SemaphoreType.DMA((6,)),
@@ -435,7 +452,7 @@
         compiler_params=pltpu.CompilerParams(
             collective_id=0, has_side_effects=True, vmem_limit_bytes=VMEM_LIMIT),
         name="decoder_layer",
-    )(prefix_owner, prefix_group, request_perm, suffix_len, rows, ln_gain_attn.reshape(1, -1),
+    )(prefix_owner, prefix_group, request_perm, suffix_len, suffix, ln_gain_attn.reshape(1, -1),
       ln_gain_mlp.reshape(1, -1), block, w3, w_out_attn, w_in, w_down)
     return jnp.transpose(out, (1, 0, 2))
 

time: 146 us -> 142 us (0.973)
  Pallas kernels: 139 us -> 136 us
  local copies, waits for them, and re-layouts: 6.87 us -> 5.14 us
    pallas_call x1, Pallas kernels: 139 us -> 136 us  [on_device(): pl.pallas_call(layer_kernel, out_shape=jax.ShapeDtypeStruct((2, 32, 2048)...]
    unnamed x2 -> x1, local copies, waits for them, and re-layouts: 4.95 us -> 3.21 us
where the time goes in v3:
time: 142 us; the launch traced here: 141 us
  Pallas kernels  136 us (96%)
  local copies, waits for them, and re-layouts  5.14 us (4%)
    pallas_call x1, Pallas kernels, on_device(): pl.pallas_call(layer_kernel, out_shape=jax.ShapeDtypeStruct((2, 32, 2048)...  136 us
    unnamed x1, local copies, waits for them, and re-layouts  3.21 us

profile of v3, /device:TPU:16, one launch (start us, length us, event | category | flops | bytes accessed | tf_op | source)
XLA Modules:
  0.0 141.4 jit_solution(10174866234171261392)
XLA Ops:
  0.0 3.2 %copy.16 = bf16[1,2048,2,256]{3,1,2,0:T(8,128)(2,1)} copy(bf16[1,2048,2,256]{3,2,1,0:T(2,128)(2,1)} %param.13) | data formatting | bytes 4194304 | tf_op args[1]
  3.2 136.3 %decoder_layer.1 = bf16[2,32,2048]{2,1,0:T(8,128)(2,1)} custom-call(s32[2]{0:T(128)} %owner_ref.1, s32[64]{0:T(128)} %group_ref.1, s32[64]{0:T(128)} %perm_ref.1, s32[64]{0:T(128)} %len_ref.1, bf16[32,2,2048]{2,1,0:T(2,128)(2,1)} %x_ref.1, f32[1,2048]{1,0:T(1,128)} %bitcast.12, f32[1,2048]{1,0:T(1,128)} %bitcast.13, bf16[2,2048,256]{2,1,0:T(8,128)(2,1)} %bitcast.9, ...), custom_call_target="tpu_custom_call" | custom-call | tf_op jit(solution)/shard_map/decoder_layer/pallas_call | solution.py:408
  139.5 1.9 %copy.14 = bf16[32,2,2048]{2,1,0:T(2,128)(2,1)} copy(bf16[32,2,2048]{2,0,1:T(8,128)(2,1)} %bitcast.11) | data formatting | bytes 524288 | tf_op jit(solution)/shard_map/transpose | solution.py:457

commit v4 on v3

--- a/solution.py
+++ b/solution.py
@@ -65,12 +65,16 @@
         due[i] = next(streams[i], None)
 
 
-def scatter_ring(wire, at, me, left, right, rooms, mix, final, times):
+def scatter_ring(wire, at, me, left, right, rooms, mix, final, times, ready=None):
     rbr, rbl, fr, fl = rooms
     opp, nxt, prv = (me + 2) % 4, (me + 1) % 4, (me + 3) % 4
+    ready = ready or (lambda i: None)
+    ready(0)
     w_rbr = wire.send(at(opp, 0), rbr, left)
     w_rbl = wire.send(at(opp, 1), rbl, right)
+    ready(1)
     w_fr1 = wire.send(at(prv, 1), fr.at[1], left)
+    ready(2)
     w_fl0 = wire.send(at(nxt, 0), fl.at[0], right)
     yield times[0]
     w_rbr()
@@ -79,6 +83,7 @@
     w_rbl()
     mix(at(nxt, 1), rbl)
     w_fl1 = wire.send(at(nxt, 1), fl.at[1], right)
+    ready(3)
     yield times[1]
     w_fr1()
     w_fl0()
@@ -177,12 +182,15 @@
         wait()
 
 
-def prefix_half(wire, p, a, kv, own, par, rooms, owner, times):
+def chunk(p, i):
+    return pl.ds(pl.multiple_of((p.y + (2, 3, 1, 0)[i]) % 4 * 512, 512), 512)
+
+
+def prefix_half(wire, p, a, kv, own, par, w_par, rooms, owner, times):
     held = owner == p.r
     chip = owner // 2 == p.r // 2
     row = owner // 8 == p.zh
     con, done = own.at[a], kv[a].at[p.core]
-    con[...] = jnp.where(held, own[a], par[a])
     yrooms, zrooms = rooms
     whose = {}
 
@@ -196,9 +204,14 @@
         into = whose["into"](whose["me"], j)
         into[...] = jnp.where(d == 0, ref[...], jnp.where(d == near_d, near[...], far[...]))
 
+    def ready(i):
+        w_par[i]()
+        rows = chunk(p, i)
+        con[rows] = jnp.where(held, con[rows], par[a, rows])
+
     yat = rows_at(con, 0, 512)
     whose.update(own=chip, at=(owner // 2) % 4, me=p.y, into=yat)
-    yield from scatter_ring(wire, yat, p.y, p.ym, p.yp, yrooms, mix, final, times[0:2])
+    yield from scatter_ring(wire, yat, p.y, p.ym, p.yp, yrooms, mix, final, times[0:2], ready)
     zat, zdone = rows_at(con, p.y * 512, 128), rows_at(done, p.y * 512, 128)
     ydone = rows_at(done, 0, 512)
     whose.update(own=row, at=owner // 8, me=p.zh, into=zdone)
@@ -322,7 +335,8 @@
         copy.start()
     greet([p.mate, p.yp, p.ym, p.zp, p.zm, p.xp, p.xm, p.zz])
     wire = Wire(ssem, rsem)
-    w_par = [wire.send(block.at[a], par.at[a], p.mate) for a in range(2)]
+    w_par = [[wire.send(block.at[a, chunk(p, i)], par.at[a, chunk(p, i)], p.mate) for i in range(4)]
+             for a in range(2)]
     for s in range(2):
         xg[s, pl.ds(pl.multiple_of(p.t * 32, 32), 32)] = normalize(x_ref[:, s, :], gain_ref[...])
     owner = owner_ref[p.core]
@@ -330,10 +344,9 @@
     def prefix(a, start, times):
         yield start
         copies[a].wait()
-        w_par[a]()
         yr, yf, zr, zf = ((yr0, yf0, zr0, zf0), (yr1, yf1, zr1, zf1))[a]
         rooms = ((yr.at[0], yr.at[1], yf.at[0], yf.at[1]), (zr.at[0], zr.at[1], zf.at[0], zf.at[1]))
-        yield from prefix_half(wire, p, a, (keys, values), own, par, rooms, owner, times)
+        yield from prefix_half(wire, p, a, (keys, values), own, par, w_par[a], rooms, owner, times)
 
     def project(start):
         yield start
@@ -389,12 +402,13 @@
         spread(inner.at[s], wd, parts.at[1, s])
         yield from scatter(s, 1, times[2])
         places = p.t * 32 + lax.broadcasted_iota(jnp.int32, (32, 2048), 0)
-        out[s] = jnp.where(places < len_ref[requests[s]], hid[s].astype(F32) + total[s], 0.0).astype(BF16)
+        total[s] = jnp.where(places < len_ref[requests[s]], hid[s].astype(F32) + total[s], 0.0)
 
     merge([
         slot(0, 0, ((13, 16, 18.5), (23, 28, 31, 33, 35), (49, 52, 54.5))),
         slot(1, 2, ((7, 12, 16.5), (22, 25, 37), (43, 48, 52.5))),
     ])
+    out[...] = jnp.stack([total[0], total[1]], axis=1).astype(BF16)
     wire.drain()
 
 
@@ -407,7 +421,7 @@
     anym = pl.BlockSpec(memory_space=pl.ANY)
     out = pl.pallas_call(
         layer_kernel,
-        out_shape=jax.ShapeDtypeStruct((2, 32, 2048), BF16),
+        out_shape=jax.ShapeDtypeStruct((32, 2, 2048), BF16),
         in_specs=[sm, sm, sm, sm, vm, vm, vm, anym, anym, anym, anym, anym],
         out_specs=vm,
         scratch_shapes=[
@@ -445,8 +459,8 @@
             pltpu.VMEM((2, 2, 256, 2048), BF16),
             pltpu.VMEM((2, 2, 256, 256), BF16),
             pltpu.VMEM((2, 2, 256, 1), F32),
-            pltpu.SemaphoreType.DMA((128,)),
-            pltpu.SemaphoreType.DMA((128,)),
+            pltpu.SemaphoreType.DMA((136,)),
+            pltpu.SemaphoreType.DMA((136,)),
             pltpu.SemaphoreType.DMA((6,)),
         ],
         compiler_params=pltpu.CompilerParams(
@@ -454,7 +468,7 @@
         name="decoder_layer",
     )(prefix_owner, prefix_group, request_perm, suffix_len, suffix, ln_gain_attn.reshape(1, -1),
       ln_gain_mlp.reshape(1, -1), block, w3, w_out_attn, w_in, w_down)
-    return jnp.transpose(out, (1, 0, 2))
+    return out
 
 
 def solution(mesh):

time: 142 us -> 140 us (0.986)
    transpose x1 -> x0, local copies, waits for them, and re-layouts: 1.92 us -> none  [on_device(): return jnp.transpose(out, (1, 0, 2))]
    unnamed x1 -> x2, local copies, waits for them, and re-layouts: 3.21 us -> 5.05 us
    pallas_call x1, Pallas kernels: 136 us -> 135 us  [on_device(): pl.pallas_call(layer_kernel, out_shape=jax.ShapeDtypeStruct((32, 2, 2048)...]
where the time goes in v4:
time: 140 us
  Pallas kernels  135 us (96%)
  local copies, waits for them, and re-layouts  5.05 us (4%)
    pallas_call x1, Pallas kernels, on_device(): pl.pallas_call(layer_kernel, out_shape=jax.ShapeDtypeStruct((32, 2, 2048)...  135 us
    unnamed x2, local copies, waits for them, and re-layouts  5.05 us

profile of v4, /device:TPU:16, one launch (start us, length us, event | category | flops | bytes accessed | tf_op | source)
XLA Modules:
  0.0 139.7 jit_solution(405514587657487633)
XLA Ops:
  0.0 3.2 %copy.15 = bf16[1,2048,2,256]{3,1,2,0:T(8,128)(2,1)} copy(bf16[1,2048,2,256]{3,2,1,0:T(2,128)(2,1)} %param.13) | data formatting | bytes 4194304 | tf_op args[1]
  3.2 134.7 %decoder_layer.1 = bf16[32,2,2048]{2,1,0:T(2,128)(2,1)} custom-call(s32[2]{0:T(128)} %owner_ref.1, s32[64]{0:T(128)} %group_ref.1, s32[64]{0:T(128)} %perm_ref.1, s32[64]{0:T(128)} %len_ref.1, bf16[32,2,2048]{2,1,0:T(2,128)(2,1)} %x_ref.1, f32[1,2048]{1,0:T(1,128)} %bitcast.10, f32[1,2048]{1,0:T(1,128)} %bitcast.11, bf16[2,2048,256]{2,1,0:T(8,128)(2,1)} %bitcast.8, ...), custom_call_target="tpu_custom_call" | custom-call | tf_op jit(solution)/shard_map/decoder_layer/pallas_call | solution.py:422
  137.9 1.8 %copy.17 = bf16[32,2,2048]{2,1,0:T(2,128)(2,1)} copy(bf16[32,2,2048]{2,1,0:T(2,128)(2,1)} %decoder_layer.1) | data formatting | bytes 524288
